TPU v7x, 256 devices: a whole 4x4x8 slice. The times are simulated.
256 devices in a mesh: seq: 8 (over y, core), fsdp: 16 (over z_hi, x), tp: 2 (over z_lo).
Axes of the slice: x: 4, y: 4, z: 8 (z_hi: 4, z_lo: 2; z = z_hi * 2 + z_lo), core: 2. Of those that a mesh axis runs over, the one named last changes fastest.
Arguments:
- hidden: bfloat16 [16, 1024, 8192], P('fsdp', 'seq'), may hold values from -6 to 6
- queries: bfloat16 [16, 1024, 8192], P('fsdp', 'seq', 'tp'), may hold values from -600 to 600
- w_kv: bfloat16 [2, 8192, 1024], P(None, 'fsdp', 'tp'), may hold values from -0.0625 to 0.0625
- b_kv: bfloat16 [2, 1024], P(None, 'tp'), may hold values from -3 to 3
- doc_starts: int32 [16, 2], P('fsdp'), may hold values from 0 to 896, as said below
- block_docs: int32 [16, 8], P('fsdp'), may hold values from 0 to 1, as said below
Outputs:
- attended: bfloat16 [16, 1024, 8192], P('fsdp', 'seq', 'tp')
Inputs may be any that keep to these rules, and one draw needn't show every extreme that they name: `doc_starts`: each row holds exactly 2 documents of whole blocks of 128 tokens, starts rising from 0; one document of each row has exactly 6 blocks. `block_docs`: the document of each block, matching doc_starts.
All inputs are finite; a program needn't handle non-finite values.
Results may differ from a plain program's by a relative error of at most 0.015.
Values may be sent and summed in bfloat16 or wider, within the bound.
A program may use at most 128 MiB of HBM per device.

v0:
```python
import jax
import jax.numpy as jnp
from jax import lax
from jax.sharding import Mesh
from jax.sharding import PartitionSpec as P

HD = 128
BLK = 128
SEQ = ("sy", "sc")
FSDP = ("fz", "fx")


def rotate_keys(key_heads, positions):
    half = key_heads.shape[-1] // 2
    freqs = jnp.exp(
        -jnp.arange(half, dtype=jnp.float32)
        * (2.0 / key_heads.shape[-1])
        * jnp.log(jnp.float32(1000000.0))
    )
    angle = positions.astype(jnp.float32)[:, None] * freqs[None, :]
    cosine = jnp.cos(angle)[:, None, :]
    sine = jnp.sin(angle)[:, None, :]
    first = key_heads[..., :half]
    second = key_heads[..., half:]
    return jnp.concatenate(
        [first * cosine - second * sine, second * cosine + first * sine], axis=-1
    )


def lookup_docs(token_index, block_table):
    block_index = token_index // BLK
    matches = block_index[:, None] == jnp.arange(block_table.shape[0], dtype=jnp.int32)[None, :]
    return jnp.sum(jnp.where(matches, block_table[None, :], 0), axis=1)


def doc_positions(token_index, doc_starts, block_docs):
    docs = lookup_docs(token_index, block_docs[0])
    doc_match = docs[:, None] == jnp.arange(doc_starts.shape[1], dtype=jnp.int32)[None, :]
    doc_first = jnp.sum(jnp.where(doc_match, doc_starts[0][None, :], 0), axis=1)
    return (docs, token_index - doc_first)


def make_per_device(cores):

    def per_device(hidden, queries, w_kv, b_kv, doc_starts, block_docs):
        tok_count = hidden.shape[1]
        core = lax.axis_index("sc")
        chip = lax.axis_index("sy")
        cols = w_kv.shape[2] // cores
        w_part = lax.dynamic_slice_in_dim(w_kv, core * cols, cols, axis=2)
        b_part = lax.dynamic_slice_in_dim(b_kv, core * cols, cols, axis=1)
        chip_rows = lax.all_gather(hidden[0], "sc", axis=0, tiled=True)
        chip_tokens = chip_rows.shape[0]
        key_value = jnp.einsum(
            "td,cde->cte",
            chip_rows,
            lax.all_gather(w_part, FSDP, axis=1, tiled=True),
            preferred_element_type=jnp.float32,
        )
        key_value = key_value + b_part.astype(jnp.float32)[:, None, :]
        chip_pos = chip * chip_tokens + jnp.arange(chip_tokens, dtype=jnp.int32)
        _, positions = doc_positions(chip_pos, doc_starts, block_docs)
        part_heads = cols // HD
        rotated = rotate_keys(key_value[0].reshape(chip_tokens, part_heads, HD), positions)
        keys = rotated.astype(jnp.bfloat16).reshape(chip_tokens, cols)
        values = key_value[1].astype(jnp.bfloat16)
        stacked = jnp.stack([keys, values])
        gathered = lax.all_gather(stacked, SEQ, axis=0, tiled=False)
        chips = gathered.shape[0] // cores
        gathered = gathered.reshape(chips, cores, 2, chip_tokens, cols)
        piece = jnp.transpose(gathered, (2, 0, 3, 1, 4)).reshape(
            2, chips * chip_tokens, cores * cols
        )
        seq_pos = (chip * cores + core) * tok_count + jnp.arange(tok_count, dtype=jnp.int32)
        query_docs = lookup_docs(seq_pos, block_docs[0])
        key_heads = piece.shape[2] // HD
        group = queries.shape[2] // HD // key_heads
        query_heads = queries[0].reshape(tok_count, key_heads, group, HD)
        inv_root = 1.0 / jnp.sqrt(jnp.float32(HD))
        width = piece.shape[1]
        key_docs = lookup_docs(jnp.arange(width, dtype=jnp.int32), block_docs[0])
        same_doc = query_docs[:, None] == key_docs[None, :]
        run_max = jnp.full((key_heads, group, tok_count), -1e30, jnp.float32)
        key_part = piece[0].reshape(width, key_heads, HD)
        value_part = piece[1].reshape(width, key_heads, HD)
        scores = (
            jnp.einsum("tgjd,sgd->gjts", query_heads, key_part, preferred_element_type=jnp.float32)
            * inv_root
        )
        scores = jnp.where(same_doc[None, None], scores, jnp.float32(-1e30))
        new_max = jnp.maximum(run_max, jnp.max(scores, axis=-1))
        weight = jnp.where(
            same_doc[None, None], jnp.exp(scores - new_max[..., None]), jnp.float32(0.0)
        )
        new_sum = jnp.sum(weight, axis=-1)
        update = jnp.einsum(
            "gjts,sgd->gjtd",
            weight.astype(jnp.bfloat16),
            value_part,
            preferred_element_type=jnp.float32,
        )
        result = update / new_sum[..., None]
        result = jnp.transpose(result, (2, 0, 1, 3)).reshape(tok_count, key_heads * group * HD)
        return result.astype(jnp.bfloat16)[None]

    return per_device


def solution(mesh):
    seq, fsdp, tp = (mesh.shape[name] for name in ("seq", "fsdp", "tp"))
    cores = 2
    x_size = 4
    fine = Mesh(
        mesh.devices.reshape(seq // cores, cores, fsdp // x_size, x_size, tp),
        ("sy", "sc", "fz", "fx", "tp"),
    )
    in_specs = (
        P(FSDP, SEQ, None),
        P(FSDP, SEQ, "tp"),
        P(None, FSDP, "tp"),
        P(None, "tp"),
        P(FSDP, None),
        P(FSDP, None),
    )
    out_specs = P(FSDP, SEQ, "tp")
    return jax.shard_map(
        make_per_device(cores), mesh=fine, in_specs=in_specs, out_specs=out_specs, check_vma=False
    )
```

profile of v0, /device:TPU:1, one launch (start us, length us, event | category | flops | bytes accessed | tf_op | source)
XLA Modules:
  0.0 223.2 jit_solution(64430388502400549)
XLA Ops:
  6.5 0.0 copy-start
  6.5 0.0 copy-start.2
  6.5 0.0 copy-start.1
  6.5 0.0 all-gather.8.cloned.1.call-start
  6.5 0.7 all-gather.8.cloned.1.call-update
  7.3 0.0 all-gather.6.cloned.1.call-start
  7.3 0.8 copy-done
  8.1 1.0 copy.37
  9.1 0.0 all-gather.6.cloned.1.call-update
  9.1 0.0 all-gather.10.cloned.1.call-start
  9.2 0.7 dynamic-slice_convert_fusion
  9.9 0.7 select_reduce_fusion.1
  10.7 0.7 fusion.24
  11.4 0.3 multiply_cosine_fusion
  11.7 21.0 %all-gather.8.cloned.1.call-done = bf16[1,256,8192]{2,1,0:T(8,128)(2,1)} async-done(((bf16[1,128,8192]{2,1,0:T(8,128)(2,1)}), bf16[1,256,8192]{2,1,0:T(8,128)(2,1)}) %all-gather.8.cloned.1.call-update) | async-done | bytes 4194320 | tf_op jit(solution)/shard_map/all_gather | solution.py:52
  32.7 127.1 %all-gather.6.cloned.1.call-done = bf16[2,8192,256]{1,2,0:T(8,128)(2,1)} async-done(((bf16[2,512,256]{1,2,0:T(8,128)(2,1)}), bf16[2,8192,256]{1,2,0:T(8,128)(2,1)}) %all-gather.6.cloned.1.call-update) | async-done | bytes 8388624 | tf_op jit(solution)/shard_map/all_gather | solution.py:57
  159.8 6.9 %fusion.14 = f32[2,256,256]{1,2,0:T(8,128)S(1)} fusion(bf16[2,8192,256]{1,2,0:T(8,128)(2,1)} %all-gather.6.cloned.1.call-done, bf16[1,256,8192]{2,1,0:T(8,128)(2,1)} %all-gather.8.cloned.1.call-done, f32[2,256]{1,0:T(2,128)S(1)} %dynamic-slice_convert_fusion), kind=kOutput, calls=%fused_computation.12 | convolution fusion | flops 2147614720 | bytes 13109248 | tf_op jit(solution)/shard_map/td,cde->cte/dot_general | solution.py:54
  166.9 0.9 copy.26
  167.8 0.0 all-gather.10.cloned.1.call-update
  167.8 0.0 copy-done.1
  167.8 1.2 copy.38
  169.0 0.0 copy-done.2
  169.0 0.1 select_reduce_fusion.2
  169.1 0.1 select_reduce_fusion
  169.2 0.2 broadcast_compare_fusion
  169.4 24.6 %all-gather.10.cloned.1.call-done = bf16[16,256,256]{2,1,0:T(8,128)(2,1)} async-done(((bf16[2,256,256]{2,1,0:T(8,128)(2,1)}), bf16[16,256,256]{2,1,0:T(8,128)(2,1)}) %all-gather.10.cloned.1.call-update) | async-done | bytes 2097168 | tf_op jit(solution)/shard_map/all_gather | solution.py:68
  194.0 3.1 %copy.27 = bf16[4,2,2,256,256]{3,0,4,1,2:T(4,128)(2,1)S(1)} copy(bf16[4,2,2,256,256]{4,3,2,1,0:T(8,128)(2,1)} %bitcast.56) | data formatting | bytes 4194304 | tf_op jit(solution)/shard_map/reshape | solution.py:70
  197.1 2.1 fusion.28
  199.2 1.8 reshape.180
  201.0 1.8 reshape_squeeze.13
  202.8 4.1 %fusion = (f32[4,8,128]{2,1,0:T(8,128)S(1)}, f32[4,1024,128,8]{2,1,3,0:T(8,128)S(1)}) fusion(pred[128,1024]{0,1:T(8,128)(4,1)S(1)} %broadcast_compare_fusion, bf16[128,4,8,128]{3,2,1,0:T(8,128)(2,1)} %bitcast.55, bf16[1024,4,128]{0,2,1:T(8,128)(2,1)S(1)} %reshape_squeeze.13), kind=kOutput, calls=%fused_computation.2 | convolution fusion | flops 1086320640 | bytes 19021824 | tf_op jit(solution)/shard_map/tgjd,sgd->gjts/dot_general | solution.py:87
  206.9 4.1 %fusion.1 = f32[4,8,128]{2,1,0:T(8,128)S(1)} fusion(f32[4,1024,128,8]{2,1,3,0:T(8,128)S(1)} %get-tuple-element.12, f32[4,8,128]{2,1,0:T(8,128)S(1)} %broadcast_maximum_fusion, pred[128,1024]{0,1:T(8,128)(4,1)S(1)} %broadcast_compare_fusion), kind=kLoop, calls=%fused_computation.3 | loop fusion | flops 20967424 | bytes 16941056 | tf_op jit(solution)/shard_map/reduce_sum | solution.py:95
  211.0 4.3 %fusion.8 = bf16[128,4,8,128]{0,3,2,1:T(8,128)(2,1)S(1)} fusion(f32[4,1024,128,8]{2,1,3,0:T(8,128)S(1)} %get-tuple-element.12, f32[4,8,128]{2,1,0:T(8,128)S(1)} %broadcast_maximum_fusion, pred[128,1024]{0,1:T(8,128)(4,1)S(1)} %broadcast_compare_fusion, bf16[1024,4,128,1]{0,2,1,3:T(8,128)(2,1)S(1)} %reshape.180, f32[128,4,8]{0,2,1:T(8,128)S(1)} %bitcast.61), kind=kOutput, calls=%fused_computation.10 | convolution fusion | flops 1095761920 | bytes 19038208 | tf_op jit(solution)/shard_map/gjts,sgd->gjtd/dot_general | solution.py:96
  215.4 1.3 copy.31
  (12 shorter events, 0.2 us)
Async XLA Ops:
  6.5 1.5 copy-start
  6.5 162.5 %copy-start.2 = (s32[1,8]{1,0:T(1,128)S(1)}, s32[1,8]{1,0:T(1,128)}, u32[]{:S(2)}) copy-start(s32[1,8]{1,0:T(1,128)} %param.11) | copy-start | bytes 100
  6.5 161.3 %copy-start.1 = (bf16[1,128,4096]{2,1,0:T(8,128)(2,1)S(1)}, bf16[1,128,4096]{2,1,0:T(8,128)(2,1)}, u32[]{:S(2)}) copy-start(bf16[1,128,4096]{2,1,0:T(8,128)(2,1)} %param.7) | copy-start | bytes 3145732
  6.5 26.1 %all-gather.8.cloned.1.call-start = ((), (), s32[]{:S(2)}) async-start(), calls=%async_computation.1 | async-start | bytes 6291456 | tf_op jit(solution)/shard_map/all_gather | solution.py:52
  7.3 152.5 %all-gather.6.cloned.1.call-start = ((), (), s32[]{:S(2)}) async-start(), calls=%async_computation | async-start | bytes 8912896 | tf_op jit(solution)/shard_map/all_gather | solution.py:57
  9.1 184.9 %all-gather.10.cloned.1.call-start = ((), (), s32[]{:S(2)}) async-start(), calls=%async_computation.2 | async-start | bytes 2359296 | tf_op jit(solution)/shard_map/all_gather | solution.py:68
Sparse Core Ops, SparseCore 0:
  9.1 23.5 all-gather.7
  35.1 124.6 all-gather.5
  167.9 26.0 all-gather.9
where the time goes:
time: 223 us
  waiting for transfers between devices  173 us (78%)
  matrix products  15.3 us (7%)
  local copies, waits for them, and re-layouts  13.9 us (6%)
  between operations  13.3 us (6%)
  other arithmetic  7.09 us (3%)
    all_gather x1, waiting for transfers between devices, per_device(): lax.all_gather(w_part, FSDP, axis=1, tiled=True)  127 us
    all_gather x1, waiting for transfers between devices, per_device(): gathered = lax.all_gather(stacked, SEQ, axis=0, tiled=False)  24.6 us
    all_gather x1, waiting for transfers between devices, per_device(): chip_rows = lax.all_gather(hidden[0], 'sc', axis=0, tiled=True)  21 us
    dot_general x1, matrix products, per_device(): jnp.einsum('td,cde->cte', chip_rows, lax.all_gather(w_part, FSDP, axis=1,...  6.93 us
  transfers between devices with their start and end apart: 3, of which 3 were waited for; matrix products, arithmetic and copies ran while one was open for 2% of the time, Pallas kernels for 0%

commit v1 on v0

--- a/solution.py
+++ b/solution.py
@@ -54,7 +54,9 @@
         key_value = jnp.einsum(
             "td,cde->cte",
             chip_rows,
-            lax.all_gather(w_part, FSDP, axis=1, tiled=True),
+            jnp.concatenate(
+                lax.all_to_all(jnp.stack([w_part] * lax.axis_size(FSDP)), FSDP, 0, 0), axis=1
+            ),
             preferred_element_type=jnp.float32,
         )
         key_value = key_value + b_part.astype(jnp.float32)[:, None, :]

time: 223 us -> 296 us (1.33)
  waiting for transfers between devices: 173 us -> 214 us
  local copies, waits for them, and re-layouts: 13.9 us -> 27.2 us
  starting transfers between devices: 0.08 us -> 11.7 us
  matrix products: 15.3 us -> 20.3 us
    all_to_all x0 -> x1, waiting for transfers between devices: none -> 182 us  [per_device(): lax.all_to_all(jnp.stack([w_part] * lax.axis_size(FSDP)), FSDP, 0, 0)]
    all_gather x1 -> x0, waiting for transfers between devices: 127 us -> none  [per_device(): lax.all_gather(w_part, FSDP, axis=1, tiled=True)]
    all_gather x1, waiting for transfers between devices: 21 us -> 0.01 us  [per_device(): chip_rows = lax.all_gather(hidden[0], 'sc', axis=0, tiled=True)]
    all_to_all x0 -> x1, starting transfers between devices: none -> 11.6 us  [per_device(): lax.all_to_all(jnp.stack([w_part] * lax.axis_size(FSDP)), FSDP, 0, 0)]
    reshape x0 -> x1, local copies, waits for them, and re-layouts: none -> 7.92 us  [per_device(): jnp.concatenate(lax.all_to_all(jnp.stack([w_part] * lax.axis_size(FSDP)),...]
    all_gather x1, waiting for transfers between devices: 24.6 us -> 31.8 us  [per_device(): gathered = lax.all_gather(stacked, SEQ, axis=0, tiled=False)]
    dot_general x1, matrix products: 4.07 us -> 9.03 us  [per_device(): jnp.einsum('tgjd,sgd->gjts', query_heads, key_part, preferred_element_typ...]
    another operation x0 -> x1, local copies, waits for them, and re-layouts: none -> 4.17 us  [per_device(): jnp.stack([w_part] * lax.axis_size(FSDP))]
  transfers between devices with their start and end apart: 3 -> 3, of which waited for: 3 -> 2; matrix products, arithmetic and copies ran while one was open for 2% -> 3% of each run, Pallas kernels for 0% -> 0%
where the time goes in v1:
time: 296 us
  waiting for transfers between devices  214 us (72%)
  local copies, waits for them, and re-layouts  27.2 us (9%)
  matrix products  20.3 us (7%)
  between operations  13.6 us (5%)
  starting transfers between devices  11.7 us (4%)
  other arithmetic  9.2 us (3%)
    all_to_all x1, waiting for transfers between devices, per_device(): lax.all_to_all(jnp.stack([w_part] * lax.axis_size(FSDP)), FSDP, 0, 0)  182 us
    all_gather x1, waiting for transfers between devices, per_device(): gathered = lax.all_gather(stacked, SEQ, axis=0, tiled=False)  31.8 us
    all_to_all x1, starting transfers between devices, per_device(): lax.all_to_all(jnp.stack([w_part] * lax.axis_size(FSDP)), FSDP, 0, 0)  11.6 us
    dot_general x1, matrix products, per_device(): jnp.einsum('tgjd,sgd->gjts', query_heads, key_part, preferred_element_typ...  9.03 us
    reduce_sum x1, other arithmetic, per_device(): new_sum = jnp.sum(weight, axis=-1)  8.22 us
    reshape x1, local copies, waits for them, and re-layouts, per_device(): jnp.concatenate(lax.all_to_all(jnp.stack([w_part] * lax.axis_size(FSDP)),...  7.92 us
    dot_general x1, matrix products, per_device(): jnp.einsum('td,cde->cte', chip_rows, jnp.concatenate(lax.all_to_all(jnp.s...  6.94 us
  transfers between devices with their start and end apart: 3, of which 2 were waited for; matrix products, arithmetic and copies ran while one was open for 3% of the time, Pallas kernels for 0%

profile of v1, /device:TPU:1, one launch (start us, length us, event | category | flops | bytes accessed | tf_op | source)
XLA Modules:
  0.0 296.0 jit_solution(13538728447720755780)
XLA Ops:
  6.5 0.0 copy-start
  6.5 0.0 copy-start.5
  6.5 0.0 copy-start.4
  6.5 0.0 copy-start.6
  6.5 1.2 copy-done
  7.8 0.2 copy.26
  8.0 4.2 %stack.4 = bf16[16,2,512,256]{2,3,1,0:T(8,128)(2,1)} broadcast(bf16[2,512,256]{1,2,0:T(8,128)(2,1)S(1)} %copy.26), dimensions={1,2,3} | broadcast | bytes 8912896 | tf_op jit(solution)/shard_map/stack | solution.py:58
  12.2 11.6 %all-to-all-start = ((bf16[16,2,512,256]{2,3,1,0:T(8,128)(2,1)}), bf16[16,2,512,256]{2,3,1,0:T(8,128)(2,1)}, u32[]{:S(2)}, u32[]{:S(2)}) async-start(bf16[16,2,512,256]{2,3,1,0:T(8,128)(2,1)} %stack.4), calls=%async_computation | async-start | bytes 16777216 | tf_op jit(solution)/shard_map/all_to_all | solution.py:58
  23.8 0.0 all-gather.5.cloned.1.call-start
  23.9 0.7 all-gather.5.cloned.1.call-update
  24.5 0.0 all-gather.7.cloned.1.call-start
  24.6 0.0 copy-done.5
  24.7 0.0 copy-done.4
  24.7 0.1 select_reduce_fusion.1
  24.8 0.0 copy-done.6
  24.8 0.1 fusion.24
  24.8 0.3 multiply_cosine_fusion
  25.2 181.6 %all-to-all-done = bf16[16,2,512,256]{2,3,1,0:T(8,128)(2,1)} async-done(((bf16[16,2,512,256]{2,3,1,0:T(8,128)(2,1)}), bf16[16,2,512,256]{2,3,1,0:T(8,128)(2,1)}, u32[]{:S(2)}, u32[]{:S(2)}) %all-to-all-start) | async-done | bytes 8388640 | tf_op jit(solution)/shard_map/all_to_all | solution.py:58
  206.7 0.0 copy-start.3
  206.7 7.9 %copy.39 = bf16[16,2,32,8,512]{4,3,0,2,1:T(8,128)(2,1)} copy(bf16[16,2,32,8,512]{4,3,2,1,0:T(8,128)(2,1)} %bitcast.18) | data formatting | bytes 16777216 | tf_op jit(solution)/shard_map/reshape | solution.py:57
  214.7 0.0 all-gather.5.cloned.1.call-done
  214.7 6.9 %fusion.14 = f32[2,256,256]{1,2,0:T(8,128)S(1)} fusion(bf16[2,8192,256]{1,2,0:T(8,128)(2,1)} %bitcast.57, bf16[1,256,8192]{2,1,0:T(8,128)(2,1)} %all-gather.5.cloned.1.call-done, f32[2,256]{1,0:T(2,128)S(1)} %dynamic-slice_convert_fusion), kind=kOutput, calls=%fused_computation.12 | convolution fusion | flops 2147614720 | bytes 13109248 | tf_op jit(solution)/shard_map/td,cde->cte/dot_general | solution.py:54
  221.8 0.9 copy.28
  222.6 0.0 all-gather.7.cloned.1.call-update
  222.7 0.0 copy-done.3
  222.7 1.2 copy.40
  223.9 0.1 select_reduce_fusion.2
  224.0 0.1 select_reduce_fusion
  224.1 0.2 broadcast_compare_fusion
  224.3 31.8 %all-gather.7.cloned.1.call-done = bf16[16,256,256]{2,1,0:T(8,128)(2,1)} async-done(((bf16[2,256,256]{2,1,0:T(8,128)(2,1)}), bf16[16,256,256]{2,1,0:T(8,128)(2,1)}) %all-gather.7.cloned.1.call-update) | async-done | bytes 2097168 | tf_op jit(solution)/shard_map/all_gather | solution.py:70
  256.1 3.1 %copy.29 = bf16[4,2,2,256,256]{3,0,4,1,2:T(4,128)(2,1)S(1)} copy(bf16[4,2,2,256,256]{4,3,2,1,0:T(8,128)(2,1)} %bitcast.60) | data formatting | bytes 4194304 | tf_op jit(solution)/shard_map/reshape | solution.py:72
  259.1 2.1 fusion.28
  261.2 0.0 copy-start.2
  261.2 1.9 reshape_squeeze.13
  263.1 9.0 %fusion = (f32[4,8,128]{2,1,0:T(8,128)S(1)}, f32[4,1024,128,8]{2,1,3,0:T(8,128)}) fusion(pred[128,1024]{0,1:T(8,128)(4,1)S(1)} %broadcast_compare_fusion, bf16[128,4,8,128]{3,2,1,0:T(8,128)(2,1)} %bitcast.59, bf16[1024,4,128]{0,2,1:T(8,128)(2,1)S(1)} %reshape_squeeze.13), kind=kOutput, calls=%fused_computation.2 | convolution fusion | flops 1086320640 | bytes 19021824 | tf_op jit(solution)/shard_map/tgjd,sgd->gjts/dot_general | solution.py:89
  272.2 0.0 copy-done.2
  272.2 0.8 reshape.190
  272.9 0.0 copy-start.1
  273.0 8.2 %fusion.1 = f32[4,8,128]{2,1,0:T(8,128)S(1)} fusion(f32[4,1024,128,8]{2,1,3,0:T(8,128)} %get-tuple-element.12, f32[4,8,128]{2,1,0:T(8,128)S(1)} %broadcast_maximum_fusion, pred[128,1024]{0,1:T(8,128)(4,1)S(1)} %broadcast_compare_fusion), kind=kLoop, calls=%fused_computation.3 | loop fusion | flops 20967424 | bytes 16941056 | tf_op jit(solution)/shard_map/reduce_sum | solution.py:97
  281.2 2.4 copy-done.1
  283.6 4.3 %fusion.8 = bf16[128,4,8,128]{0,3,2,1:T(8,128)(2,1)S(1)} fusion(f32[4,1024,128,8]{2,1,3,0:T(8,128)S(1)} %copy-done.1, f32[4,8,128]{2,1,0:T(8,128)S(1)} %broadcast_maximum_fusion, pred[128,1024]{0,1:T(8,128)(4,1)S(1)} %broadcast_compare_fusion, bf16[1024,4,128,1]{0,2,1,3:T(8,128)(2,1)S(1)} %reshape.190, f32[128,4,8]{0,2,1:T(8,128)S(1)} %bitcast.65), kind=kOutput, calls=%fused_computation.10 | convolution fusion | flops 1095761920 | bytes 19038208 | tf_op jit(solution)/shard_map/gjts,sgd->gjtd/dot_general | solution.py:98
  287.9 1.3 copy.33
  (13 shorter events, 0.2 us)
Async XLA Ops:
  6.5 1.2 copy-start
  6.5 18.1 %copy-start.5 = (bf16[2,512]{1,0:T(2,128)(2,1)S(1)}, bf16[2,512]{1,0:T(2,128)(2,1)}, u32[]{:S(2)}) copy-start(bf16[2,512]{1,0:T(2,128)(2,1)} %param.9) | copy-start | bytes 6148
  6.5 18.1 %copy-start.4 = (s32[1,8]{1,0:T(1,128)S(1)}, s32[1,8]{1,0:T(1,128)}, u32[]{:S(2)}) copy-start(s32[1,8]{1,0:T(1,128)} %param.11) | copy-start | bytes 100
  6.5 18.2 %copy-start.6 = (s32[1,2]{1,0:T(1,128)S(1)}, s32[1,2]{1,0:T(1,128)}, u32[]{:S(2)}) copy-start(s32[1,2]{1,0:T(1,128)} %param.10) | copy-start | bytes 28
  12.2 194.6 %all-to-all-start = ((bf16[16,2,512,256]{2,3,1,0:T(8,128)(2,1)}), bf16[16,2,512,256]{2,3,1,0:T(8,128)(2,1)}, u32[]{:S(2)}, u32[]{:S(2)}) async-start(bf16[16,2,512,256]{2,3,1,0:T(8,128)(2,1)} %stack.4), calls=%async_computation | async-start | bytes 16777216 | tf_op jit(solution)/shard_map/all_to_all | solution.py:58
  23.8 190.9 %all-gather.5.cloned.1.call-start = ((), (), s32[]{:S(2)}) async-start(), calls=%async_computation.1 | async-start | bytes 6291456 | tf_op jit(solution)/shard_map/all_gather | solution.py:52
  24.5 231.5 %all-gather.7.cloned.1.call-start = ((), (), s32[]{:S(2)}) async-start(), calls=%async_computation.2 | async-start | bytes 2359296 | tf_op jit(solution)/shard_map/all_gather | solution.py:70
  206.7 15.9 %copy-start.3 = (bf16[1,128,4096]{2,1,0:T(8,128)(2,1)S(1)}, bf16[1,128,4096]{2,1,0:T(8,128)(2,1)}, u32[]{:S(2)}) copy-start(bf16[1,128,4096]{2,1,0:T(8,128)(2,1)} %param.7) | copy-start | bytes 3145732
  261.2 10.9 %copy-start.2 = (bf16[1,4,256,2,256]{2,1,4,3,0:T(4,128)(2,1)S(1)}, bf16[1,4,256,2,256]{2,1,4,3,0:T(4,128)(2,1)}, u32[]{:S(2)}) copy-start(bf16[1,4,256,2,256]{2,1,4,3,0:T(4,128)(2,1)} %get-tuple-element.5) | copy-start | bytes 3145732
  272.9 10.6 %copy-start.1 = (f32[4,1024,128,8]{2,1,3,0:T(8,128)S(1)}, f32[4,1024,128,8]{2,1,3,0:T(8,128)}, u32[]{:S(2)}) copy-start(f32[4,1024,128,8]{2,1,3,0:T(8,128)} %get-tuple-element.12) | copy-start | bytes 50331652
Sparse Core Ops, SparseCore 0:
  26.4 21.4 all-gather.4
  222.8 33.2 all-gather.6
